TPU v7x, 1024 devices: a whole 8x8x8 slice. The times are simulated.
1024 devices in a mesh: row: 32 (over y, x_hi), col: 32 (over x_lo, z, core).
Axes of the slice: x: 8 (x_hi: 4, x_lo: 2; x = x_hi * 2 + x_lo), y: 8, z: 8, core: 2. Of those that a mesh axis runs over, the one named last changes fastest.
Arguments:
- activations: bfloat16 [256, 8192], P('col', 'row'), may hold values from -6 to 6
- out_grad: bfloat16 [256, 8192], P('col', 'row'), may hold values from -6 to 6
- w_gate: bfloat16 [8192, 28672], P('row', 'col'), may hold values from -0.0625 to 0.0625
- w_up: bfloat16 [8192, 28672], P('row', 'col'), may hold values from -0.0625 to 0.0625
- w_down: bfloat16 [28672, 8192], P('col', 'row'), may hold values from -0.03125 to 0.03125
Outputs:
- grad_input: bfloat16 [256, 8192], P('col', 'row')
- grad_w_gate: bfloat16 [8192, 28672], P('row', 'col')
- grad_w_up: bfloat16 [8192, 28672], P('row', 'col')
- grad_w_down: bfloat16 [28672, 8192], P('col', 'row')
All inputs are finite; a program needn't handle non-finite values.
Results may differ from a plain program's by a relative error of at most 0.0049.
Values may be sent and summed in bfloat16 or wider, within the bound.
A program may use at most 32 MiB of HBM per device.

v0:
```python
import jax
import jax.numpy as jnp
from jax import lax
from jax.sharding import PartitionSpec as P


def swiglu_backward(sums, width):
    gate = sums[:, :width]
    upward = sums[:, width : 2 * width]
    back = sums[:, 2 * width :]
    sigma = jax.nn.sigmoid(gate)
    hidden = (gate * sigma * upward).astype(jnp.bfloat16)
    grad_gate = (back * upward * sigma * (1.0 + gate * (1.0 - sigma))).astype(jnp.bfloat16)
    grad_up = (back * gate * sigma).astype(jnp.bfloat16)
    return (hidden, grad_gate, grad_up)


def per_device(activations, out_grad, w_gate, w_up, w_down):
    tokens_all, grads_all = (
        lax.all_gather(activations, "col", axis=0, tiled=True),
        lax.all_gather(out_grad, "col", axis=0, tiled=True),
    )
    width = w_gate.shape[1]
    contract_last = (((1,), (1,)), ((), ()))
    contract_first = (((0,), (0,)), ((), ()))
    gate = jnp.dot(tokens_all, w_gate, preferred_element_type=jnp.float32)
    upward = jnp.dot(tokens_all, w_up, preferred_element_type=jnp.float32)
    back = lax.dot_general(grads_all, w_down, contract_last, preferred_element_type=jnp.float32)
    shares = lax.psum_scatter(
        jnp.concatenate([gate, upward, back], axis=1), "row", scatter_dimension=0, tiled=True
    )
    hidden_part, gate_part, up_part = swiglu_backward(shares, width)
    hidden, grad_gate, grad_up = (
        lax.all_gather(hidden_part, "row", axis=0, tiled=True),
        lax.all_gather(gate_part, "row", axis=0, tiled=True),
        lax.all_gather(up_part, "row", axis=0, tiled=True),
    )
    result = lax.dot_general(grad_gate, w_gate, contract_last, preferred_element_type=jnp.float32)
    grad_input = lax.psum_scatter(
        result + lax.dot_general(grad_up, w_up, contract_last, preferred_element_type=jnp.float32),
        "col",
        scatter_dimension=0,
        tiled=True,
    ).astype(jnp.bfloat16)
    grad_w_gate = lax.dot_general(
        tokens_all, grad_gate, contract_first, preferred_element_type=jnp.float32
    ).astype(jnp.bfloat16)
    grad_w_up = lax.dot_general(
        tokens_all, grad_up, contract_first, preferred_element_type=jnp.float32
    ).astype(jnp.bfloat16)
    grad_w_down = lax.dot_general(
        hidden, grads_all, contract_first, preferred_element_type=jnp.float32
    ).astype(jnp.bfloat16)
    return (grad_input, grad_w_gate, grad_w_up, grad_w_down)


def solution(mesh):
    in_specs = (P("col", "row"), P("col", "row"), P("row", "col"), P("row", "col"), P("col", "row"))
    out_specs = (P("col", "row"), P("row", "col"), P("row", "col"), P("col", "row"))
    return jax.shard_map(
        per_device, mesh=mesh, in_specs=in_specs, out_specs=out_specs, check_vma=False
    )
```

profile of v0, /device:TPU:1, one launch (start us, length us, event | category | flops | bytes accessed | tf_op | source)
XLA Modules:
  0.0 711.9 jit_solution(16062563941856685534)
XLA Ops:
  7.2 0.0 all-reduce.3.cloned.1.call-start
  7.2 48.8 %all_gather.15 = bf16[256,256]{1,0:T(8,128)(2,1)S(1)} all-gather(bf16[8,256]{1,0:T(8,128)(2,1)} %param.5), channel_id=1, replica_groups=mesh['row'=32,'col'=32] {'col'}, dimensions={0}, use_global_device_ids=true | all-gather | bytes 135168 | tf_op jit(solution)/shard_map/all_gather | solution.py:20
  56.0 0.3 fusion.2
  56.3 1.3 fusion.3
  57.6 31.1 %all_gather.16 = bf16[256,256]{1,0:T(8,128)(2,1)S(1)} all-gather(bf16[8,256]{1,0:T(8,128)(2,1)S(1)} %copy-done.3), channel_id=1, replica_groups=mesh['row'=32,'col'=32] {'col'}, dimensions={0}, use_global_device_ids=true | all-gather | bytes 135168 | tf_op jit(solution)/shard_map/all_gather | solution.py:21
  88.7 0.3 fusion.4
  89.0 1.8 pad_maximum_fusion
  90.8 0.0 reduce-scatter.2.cloned.1.call-start
  90.9 1.3 dynamic-slice
  92.8 312.2 %all-reduce.3.cloned.1.call-done = f32[256,2688]{1,0:T(8,128)} async-done(((f32[256,2688]{1,0:T(8,128)}), f32[256,2688]{1,0:T(8,128)}) %all-reduce.3.cloned.1.call-update) | async-done | bytes 2752528
  405.0 0.9 multiply_convert_fusion
  406.0 65.7 %all_gather.17 = bf16[256,896]{1,0:T(8,128)(2,1)S(1)} all-gather(bf16[8,896]{1,0:T(8,128)(2,1)S(1)} %get-tuple-element.13), channel_id=1, replica_groups=mesh['row'=32,'col'=32] {'row'}, dimensions={0}, use_global_device_ids=true | all-gather | bytes 473088 | tf_op jit(solution)/shard_map/all_gather | solution.py:35
  471.6 0.3 fusion.5
  472.0 0.3 fusion
  472.3 66.9 %all_gather.18 = bf16[256,896]{1,0:T(8,128)(2,1)S(1)} all-gather(bf16[8,896]{1,0:T(8,128)(2,1)S(1)} %get-tuple-element.14), channel_id=1, replica_groups=mesh['row'=32,'col'=32] {'row'}, dimensions={0}, use_global_device_ids=true | all-gather | bytes 473088 | tf_op jit(solution)/shard_map/all_gather | solution.py:36
  539.2 1.0 convolution_add_fusion
  540.3 0.0 reduce-scatter.2.cloned.1.call-update
  540.3 0.3 fusion.1
  540.6 1.0 copy.11
  541.6 1.0 copy.12
  542.6 64.6 %all_gather.19 = bf16[256,896]{1,0:T(8,128)(2,1)S(1)} all-gather(bf16[8,896]{1,0:T(8,128)(2,1)S(1)} %get-tuple-element.12), channel_id=1, replica_groups=mesh['row'=32,'col'=32] {'row'}, dimensions={0}, use_global_device_ids=true | all-gather | bytes 473088 | tf_op jit(solution)/shard_map/all_gather | solution.py:34
  607.2 1.1 convolution_convert_fusion
  608.3 95.5 %reduce-scatter.2.cloned.1.call-done = f32[8,256]{1,0:T(8,128)} async-done(((f32[256,256]{1,0:T(8,128)}), f32[8,256]{1,0:T(8,128)}) %reduce-scatter.2.cloned.1.call-update) | async-done | bytes 8208 | tf_op jit(solution)/shard_map/reduce_scatter | solution.py:39
  703.8 1.3 convert_element_type.29
  (9 shorter events, 0.0 us)
Async XLA Ops:
  7.2 48.8 %copy-start = (bf16[256,896]{1,0:T(8,128)(2,1)S(1)}, bf16[256,896]{1,0:T(8,128)(2,1)}, u32[]{:S(2)}) copy-start(bf16[256,896]{1,0:T(8,128)(2,1)} %param.7) | copy-start | bytes 1376260
  7.2 50.4 %copy-start.3 = (bf16[8,256]{1,0:T(8,128)(2,1)S(1)}, bf16[8,256]{1,0:T(8,128)(2,1)}, u32[]{:S(2)}) copy-start(bf16[8,256]{1,0:T(8,128)(2,1)} %param.6) | copy-start | bytes 12292
  7.2 81.5 %copy-start.2 = (bf16[896,256]{1,0:T(8,128)(2,1)S(1)}, bf16[896,256]{1,0:T(8,128)(2,1)}, u32[]{:S(2)}) copy-start(bf16[896,256]{1,0:T(8,128)(2,1)} %param.9) | copy-start | bytes 1376260
  7.2 397.8 %all-reduce.3.cloned.1.call-start = ((), (), s32[]{:S(2)}) async-start(), calls=%async_computation.2 | async-start | bytes 5505024
  90.8 448.5 %copy-start.1 = (bf16[256,896]{1,0:T(8,128)(2,1)S(1)}, bf16[256,896]{1,0:T(8,128)(2,1)}, u32[]{:S(2)}) copy-start(bf16[256,896]{1,0:T(8,128)(2,1)} %param.8) | copy-start | bytes 1376260
  90.8 613.0 %reduce-scatter.2.cloned.1.call-start = ((), (), s32[]{:S(2)}) async-start(), calls=%async_computation.1 | async-start | bytes 270336 | tf_op jit(solution)/shard_map/reduce_scatter | solution.py:39
Sparse Core Ops, SparseCore 0:
  90.9 314.0 all-reduce.2
  540.4 163.3 reduce-scatter.1
where the time goes:
time: 715 us; the launch traced here: 712 us
  waiting for transfers between devices  408 us (57%)
  blocking collectives  277 us (39%)
  between operations  14.8 us (2%)
    unnamed x3, waiting for transfers between devices  312 us
    reduce_scatter x1, waiting for transfers between devices, per_device(): lax.psum_scatter(result + lax.dot_general(grad_up, w_up, contract_last, p...  95.5 us
    all_gather x1, blocking collectives, per_device(): lax.all_gather(up_part, 'row', axis=0, tiled=True)  66.9 us
    all_gather x1, blocking collectives, per_device(): lax.all_gather(gate_part, 'row', axis=0, tiled=True)  65.7 us
    all_gather x1, blocking collectives, per_device(): lax.all_gather(hidden_part, 'row', axis=0, tiled=True)  64.6 us
    all_gather x1, blocking collectives, per_device(): lax.all_gather(activations, 'col', axis=0, tiled=True)  48.8 us
    all_gather x1, blocking collectives, per_device(): lax.all_gather(out_grad, 'col', axis=0, tiled=True)  31.1 us
  transfers between devices with their start and end apart: 2, of which 2 were waited for; matrix products, arithmetic and copies ran while one was open for 1% of the time, Pallas kernels for 0%

commit v1 on v0

v1 whole, which is shorter than its diff:
```python
import functools

import jax
import jax.numpy as jnp
from jax import lax
from jax.experimental import pallas as pl
from jax.experimental.pallas import tpu as pltpu
from jax.sharding import PartitionSpec as P

MESH = pl.DeviceIdType.MESH
F32 = jnp.float32
BF16 = jnp.bfloat16

NY, NX, NZ = 8, 4, 8


def flat(value):
    n, rows, width = value.shape
    return value.astype(F32).reshape(n * rows, width).astype(BF16)


def kernel(
    act_ref, og_ref, wg_hbm, wu_hbm, wd_hbm,
    gi_ref, gwg_ref, gwu_ref, gwd_ref,
    wg, wu, wd, xbuf, tok, grd, part, rbuf, xrecv, hbuf, gpart, gsend, grecv,
    w_sem, a_send, a_recv, c_send, c_recv, x_send, x_recv, h_send, h_recv, d_send, d_recv, e_send, e_recv,
):
    row, col = lax.axis_index("row"), lax.axis_index("col")
    y, xh = row // NX, row % NX
    xl, z, core = col // (2 * NZ), (col // 2) % NZ, col % 2

    loads = [pltpu.make_async_copy(src, dst, w_sem.at[i]) for i, (src, dst) in enumerate(((wg_hbm, wg), (wu_hbm, wu), (wd_hbm, wd)))]
    for load in loads:
        load.start()

    def col_peer(slot):
        dx, dz, dc = slot // (2 * NZ), (slot // 2) % NZ, slot % 2
        peer = ((xl + dx) % 2) * (2 * NZ) + ((z + dz) % NZ) * 2 + (core + dc) % 2
        return peer, dx * (2 * NZ) + ((NZ - dz) % NZ) * 2 + dc

    def row_id(yy, xx):
        return (yy * NX + xx, col)

    barrier = pltpu.get_barrier_semaphore()

    def greet(slot, carry):
        peer, _ = col_peer(slot)
        pl.semaphore_signal(barrier, inc=1, device_id=(row, peer), device_id_type=MESH)
        return carry

    lax.fori_loop(1, 32, greet, 0)
    for t in range(NX - 1):
        pl.semaphore_signal(barrier, inc=1, device_id=row_id(y, (xh + 1 + t) % NX), device_id_type=MESH)
    for step in (1, NY - 1):
        pl.semaphore_signal(barrier, inc=1, device_id=row_id((y + step) % NY, xh), device_id_type=MESH)
    xbuf[0, 0] = act_ref[...]
    xbuf[0, 1] = og_ref[...]
    pl.semaphore_wait(barrier, 31 + (NX - 1) + 2)

    def gather_copy(slot):
        peer, there = col_peer(slot)
        return pltpu.make_async_remote_copy(
            src_ref=xbuf.at[0], dst_ref=xbuf.at[there], send_sem=a_send.at[slot], recv_sem=a_recv.at[there],
            device_id=(row, peer), device_id_type=MESH,
        )

    def gather_start(slot, carry):
        gather_copy(slot).start()
        return carry

    lax.fori_loop(1, 32, gather_start, 0)

    def gather_wait(slot, carry):
        pltpu.make_async_remote_copy(
            src_ref=xbuf.at[0], dst_ref=xbuf.at[slot], send_sem=a_send.at[slot], recv_sem=a_recv.at[slot],
            device_id=(row, col_peer(slot)[0]), device_id_type=MESH,
        ).wait()
        return carry

    lax.fori_loop(1, 32, gather_wait, 0)
    tok[...] = flat(xbuf[:, 0])
    grd[...] = flat(xbuf[:, 1])

    for load in loads:
        load.wait()
    part[:, 0] = jnp.dot(tok[...], wg[...], preferred_element_type=F32).reshape(32, 8, -1)
    part[:, 1] = jnp.dot(tok[...], wu[...], preferred_element_type=F32).reshape(32, 8, -1)
    part[:, 2] = lax.dot_general(grd[...], wd[...], (((1,), (1,)), ((), ())), preferred_element_type=F32).reshape(32, 8, -1)

    def chain(side, k, t, src):
        return pltpu.make_async_remote_copy(
            src_ref=src, dst_ref=rbuf.at[side, k - 1, t],
            send_sem=c_send.at[side, k - 1, t], recv_sem=c_recv.at[side, k - 1, t],
            device_id=row_id((y + (1 if side == 0 else NY - 1)) % NY, xh), device_id_type=MESH,
        )

    def far(side, t):
        return (t < 2) == (side == 0)

    sent = []
    for k in (4, 3, 2, 1):
        for t in range(NX):
            for side in (0, 1):
                if k == 4 and not far(side, t):
                    continue
                block = ((y + (k if side == 0 else NY - k)) % NY) * NX + (xh + 1 + t) % NX
                if k <= 2 or (k == 3 and far(side, t)):
                    held = rbuf.at[side, k, t]
                    chain(side, k + 1, t, held).wait_recv()
                    held[...] += part[block]
                    copy = chain(side, k, t, held)
                else:
                    copy = chain(side, k, t, part.at[block])
                copy.start()
                sent.append(copy)

    for t in range(NX):
        for side in (0, 1):
            chain(side, 1, t, rbuf.at[side, 0, t]).wait_recv()
        total = rbuf.at[0, 0, t]
        total[...] += rbuf[1, 0, t] + part[y * NX + (xh + 1 + t) % NX]
        if t < NX - 1:
            copy = pltpu.make_async_remote_copy(
                src_ref=total, dst_ref=xrecv.at[t], send_sem=x_send.at[t], recv_sem=x_recv.at[t],
                device_id=row_id(y, (xh + 1 + t) % NX), device_id_type=MESH,
            )
            copy.start()
            sent.append(copy)
    for t in range(NX - 1):
        pltpu.make_async_remote_copy(
            src_ref=xrecv.at[t], dst_ref=xrecv.at[t], send_sem=x_send.at[t], recv_sem=x_recv.at[t],
            device_id=row_id(y, (xh + NX - 1 - t) % NX), device_id_type=MESH,
        ).wait_recv()
    sums = rbuf[0, 0, NX - 1] + xrecv[0] + xrecv[1] + xrecv[2]
    gate, upward, back = sums[0], sums[1], sums[2]
    sigma = jax.nn.sigmoid(gate)
    mine = y * NX + xh
    hbuf[mine, 0] = (gate * sigma * upward).astype(BF16)
    hbuf[mine, 1] = (back * upward * sigma * (1.0 + gate * (1.0 - sigma))).astype(BF16)
    hbuf[mine, 2] = (back * gate * sigma).astype(BF16)

    def share(t, block):
        return pltpu.make_async_remote_copy(
            src_ref=hbuf.at[block], dst_ref=hbuf.at[block], send_sem=h_send.at[t], recv_sem=h_recv.at[t],
            device_id=row_id(y, (xh + 1 + t) % NX), device_id_type=MESH,
        )

    def forward(side, k, u, block):
        return pltpu.make_async_remote_copy(
            src_ref=hbuf.at[block], dst_ref=hbuf.at[block],
            send_sem=d_send.at[side, k - 1, u], recv_sem=d_recv.at[side, k - 1, u],
            device_id=row_id((y + (1 if side == 0 else NY - 1)) % NY, xh), device_id_type=MESH,
        )

    def source(side, k, u):
        return ((y + (NY - k if side == 0 else k)) % NY) * NX + (xh + NX - u) % NX

    for t in range(NX - 1):
        copy = share(t, mine)
        copy.start()
        sent.append(copy)
    for k in (1, 2, 3, 4):
        for u in (0, 1, 3, 2):
            if k == 1 and u > 0:
                share(u - 1, source(0, 0, u)).wait_recv()
            for side in (0, 1):
                if k == 4 and not far(side, u):
                    continue
                block = source(side, k - 1, u)
                if k > 1:
                    forward(side, k - 1, u, block).wait_recv()
                copy = forward(side, k, u, block)
                copy.start()
                sent.append(copy)
    for side in (0, 1):
        for u in range(NX):
            last = 4 if far(side, u) else 3
            forward(side, last, u, source(side, last, u)).wait_recv()

    last_dims = (((1,), (1,)), ((), ()))
    first_dims = (((0,), (0,)), ((), ()))
    grad_gate, grad_up = flat(hbuf[:, 1]), flat(hbuf[:, 2])
    gpart[...] = (
        lax.dot_general(grad_gate, wg[...], last_dims, preferred_element_type=F32)
        + lax.dot_general(grad_up, wu[...], last_dims, preferred_element_type=F32)
    ).reshape(32, 8, -1)
    gsend[...] = gpart[...].astype(BF16)

    def return_start(slot, carry):
        peer, there = col_peer(slot)
        pltpu.make_async_remote_copy(
            src_ref=gsend.at[slot], dst_ref=grecv.at[there], send_sem=e_send.at[slot], recv_sem=e_recv.at[there],
            device_id=(row, peer), device_id_type=MESH,
        ).start()
        return carry

    lax.fori_loop(1, 32, return_start, 0)
    gwg_ref[...] = lax.dot_general(tok[...], grad_gate, first_dims, preferred_element_type=F32).astype(BF16)
    gwu_ref[...] = lax.dot_general(tok[...], grad_up, first_dims, preferred_element_type=F32).astype(BF16)
    gwd_ref[...] = lax.dot_general(flat(hbuf[:, 0]), grd[...], first_dims, preferred_element_type=F32).astype(BF16)

    def return_wait(slot, total):
        pltpu.make_async_remote_copy(
            src_ref=gsend.at[slot], dst_ref=grecv.at[slot], send_sem=e_send.at[slot], recv_sem=e_recv.at[slot],
            device_id=(row, col_peer(slot)[0]), device_id_type=MESH,
        ).wait()
        return total + grecv[slot].astype(F32)

    gi_ref[...] = lax.fori_loop(1, 32, return_wait, gpart[0]).astype(BF16)
    for copy in sent:
        copy.wait_send()


def per_device(activations, out_grad, w_gate, w_up, w_down):
    depth, width = w_gate.shape
    dma = pltpu.SemaphoreType.DMA
    vmem = pl.BlockSpec(memory_space=pltpu.VMEM)
    return pl.pallas_call(
        kernel,
        out_shape=(
            jax.ShapeDtypeStruct((8, depth), BF16),
            jax.ShapeDtypeStruct((depth, width), BF16),
            jax.ShapeDtypeStruct((depth, width), BF16),
            jax.ShapeDtypeStruct((width, depth), BF16),
        ),
        in_specs=[vmem, vmem] + [pl.BlockSpec(memory_space=pl.ANY)] * 3,
        out_specs=(vmem,) * 4,
        scratch_shapes=[
            pltpu.VMEM((depth, width), BF16),
            pltpu.VMEM((depth, width), BF16),
            pltpu.VMEM((width, depth), BF16),
            pltpu.VMEM((32, 2, 8, depth), BF16),
            pltpu.VMEM((256, depth), BF16),
            pltpu.VMEM((256, depth), BF16),
            pltpu.VMEM((32, 3, 8, width), F32),
            pltpu.VMEM((2, 4, NX, 3, 8, width), F32),
            pltpu.VMEM((NX - 1, 3, 8, width), F32),
            pltpu.VMEM((32, 3, 8, width), BF16),
            pltpu.VMEM((32, 8, depth), F32),
            pltpu.VMEM((32, 8, depth), BF16),
            pltpu.VMEM((32, 8, depth), BF16),
            dma((3,)),
            dma((32,)), dma((32,)),
            dma((2, 4, NX)), dma((2, 4, NX)),
            dma((NX - 1,)), dma((NX - 1,)),
            dma((NX - 1,)), dma((NX - 1,)),
            dma((2, 4, NX)), dma((2, 4, NX)),
            dma((32,)), dma((32,)),
        ],
        compiler_params=pltpu.CompilerParams(collective_id=0, has_side_effects=True, vmem_limit_bytes=48 << 20),
        name="ffn_backward",
    )(activations, out_grad, w_gate, w_up, w_down)


def solution(mesh):
    in_specs = (P("col", "row"), P("col", "row"), P("row", "col"), P("row", "col"), P("col", "row"))
    out_specs = (P("col", "row"), P("row", "col"), P("row", "col"), P("col", "row"))
    return jax.shard_map(
        per_device, mesh=mesh, in_specs=in_specs, out_specs=out_specs, check_vma=False
    )
```

time: 715 us -> 107 us (0.15)
  waiting for transfers between devices: 408 us -> 0 us
  blocking collectives: 277 us -> 0 us
  Pallas kernels: 0 us -> 97.8 us
  between operations: 14.8 us -> 0.65 us
    unnamed x3 -> x0, waiting for transfers between devices: 312 us -> none
    all_gather x5 -> x0, blocking collectives: 277 us -> none  [the longest x1 66.9 us: per_device(): lax.all_gather(up_part, 'row', axis=0, tiled=True)]
    pallas_call x0 -> x1, Pallas kernels: none -> 97.8 us  [per_device(): pl.pallas_call(kernel, out_shape=(jax.ShapeDtypeStruct((8, depth), BF16),...]
    reduce_scatter x1 -> x0, waiting for transfers between devices: 95.5 us -> none  [per_device(): lax.psum_scatter(result + lax.dot_general(grad_up, w_up, contract_last, p...]
  transfers between devices with their start and end apart: 2 -> 0, of which waited for: 2 -> 0; matrix products, arithmetic and copies ran while one was open for 1% -> 0% of each run, Pallas kernels for 0% -> 0%
where the time goes in v1:
time: 107 us; the launch traced here: 106 us
  Pallas kernels  97.8 us (91%)
  local copies, waits for them, and re-layouts  7.32 us (7%)
    pallas_call x1, Pallas kernels, per_device(): pl.pallas_call(kernel, out_shape=(jax.ShapeDtypeStruct((8, depth), BF16),...  97.8 us
    unnamed x14, local copies, waits for them, and re-layouts  7.32 us

profile of v1, /device:TPU:1, one launch (start us, length us, event | category | flops | bytes accessed | tf_op | source)
XLA Modules:
  0.0 105.8 jit_solution(6271315308256577802)
XLA Ops:
  0.6 0.0 copy-start
  0.6 1.0 copy-done
  1.7 0.0 copy-start.1
  1.7 1.0 copy-done.1
  2.7 0.0 copy-start.2
  2.7 1.0 copy-done.2
  3.7 0.0 copy-start.3
  3.7 0.7 copy-done.3
  4.4 0.0 copy-start.4
  4.4 0.7 copy-done.4
  5.1 97.8 %ffn_backward.1 = (bf16[8,256]{1,0:T(8,128)(2,1)S(1)}, bf16[256,896]{1,0:T(8,128)(2,1)S(1)}, bf16[256,896]{1,0:T(8,128)(2,1)S(1)}, bf16[896,256]{1,0:T(8,128)(2,1)S(1)}) custom-call(bf16[8,256]{1,0:T(8,128)(2,1)S(1)} %copy-done.3, bf16[8,256]{1,0:T(8,128)(2,1)S(1)} %copy-done.4, bf16[256,896]{1,0:T(8,128)(2,1)S(1)} %copy-done, ...), custom_call_target="tpu_custom_call" | custom-call | tf_op jit(solution)/shard_map/ffn_backward/pallas_call | solution.py:218
  102.9 0.6 copy.13
  103.4 0.8 copy.14
  104.2 0.8 copy.15
  105.0 0.8 copy.16
Async XLA Ops:
  0.6 1.0 copy-start
  1.7 1.0 copy-start.1
  2.7 1.0 copy-start.2
  3.7 0.7 copy-start.3
  4.4 0.7 copy-start.4

commit v2 on v0

v2 whole, which is shorter than its diff:
```python
import functools

import jax
import jax.numpy as jnp
from jax import lax
from jax.experimental import pallas as pl
from jax.experimental.pallas import tpu as pltpu
from jax.sharding import PartitionSpec as P

MESH = pl.DeviceIdType.MESH
F32 = jnp.float32
BF16 = jnp.bfloat16

NY, NX, NZ = 8, 4, 8
LAST_DIMS = (((1,), (1,)), ((), ()))
FIRST_DIMS = (((0,), (0,)), ((), ()))


def flat(value):
    n, rows, width = value.shape
    return value.astype(F32).reshape(n * rows, width).astype(BF16)


def far(side, t):
    return (t < 2) == (side == 0)


def narrow(side, k, t):
    return k >= 3 or (k == 2 and not far(side, t))


def kernel(
    bounds,
    act_hbm, og_hbm, wg_hbm, wu_hbm, wd_hbm,
    gi_hbm, gwg_hbm, gwu_hbm, gwd_hbm,
    gi_ref, gwg_ref, gwu_ref, gwd_ref, wg, wu, wd, xbuf, tok, grd, gpart, gcore, gcore_in, gline, gline_in, gown, gown_in,
    w_sem, o_sem, a_send, a_recv, c_send, c_recv, x_send, x_recv, h_send, h_recv, d_send, d_recv, e_send, e_recv,
    *parts,
):
    row, col = lax.axis_index("row"), lax.axis_index("col")
    y, xh = row // NX, row % NX
    xl, z, core = col // (2 * NZ), (col // 2) % NZ, col % 2
    mine = y * NX + xh
    halves = [parts[7 * h : 7 * h + 7] for h in range(len(bounds))]

    def col_id(dx, dz, dc):
        return (row, ((xl + dx) % 2) * (2 * NZ) + ((z + dz) % NZ) * 2 + (core + dc) % 2)

    def row_id(dy, dx):
        return (((y + dy) % NY) * NX + (xh + dx) % NX, col)

    sent = []

    def remote(src, dst, send, recv, device, start=True):
        copy = pltpu.make_async_remote_copy(
            src_ref=src, dst_ref=dst, send_sem=send, recv_sem=recv, device_id=device, device_id_type=MESH
        )
        if start:
            copy.start()
            sent.append(copy)
        return copy

    own = [
        pltpu.make_async_copy(act_hbm, xbuf.at[0, 0], w_sem.at[0]),
        pltpu.make_async_copy(og_hbm, xbuf.at[0, 1], w_sem.at[1]),
    ]
    loads = [
        pltpu.make_async_copy(src, dst, w_sem.at[2 + i])
        for i, (src, dst) in enumerate(((wg_hbm, wg), (wu_hbm, wu), (wd_hbm, wd)))
    ]
    for load in own + loads:
        load.start()

    barrier = pltpu.get_barrier_semaphore()
    partners = [col_id(0, dz, 0) for dz in range(1, NZ)] + [col_id(1, 0, 0), col_id(0, 0, 1)]
    partners += [row_id(1, 0), row_id(NY - 1, 0)] + [row_id(0, dx) for dx in range(1, NX)]
    for partner in partners:
        pl.semaphore_signal(barrier, inc=1, device_id=partner, device_id_type=MESH)
    for load in own:
        load.wait()
    pl.semaphore_wait(barrier, len(partners))

    def gather(slot, there, device, start=True):
        return remote(xbuf.at[slot], xbuf.at[there], a_send.at[there], a_recv.at[there], device, start)

    def arrived(slot):
        gather(slot, slot, col_id(0, 0, 1), start=False).wait_recv()

    def to_core(slot):
        gather(slot, slot + 1, col_id(0, 0, 1))

    order = (1, 7, 2, 6, 3, 5, 4)
    for dz in order:
        gather(0, (NZ - dz) * 2, col_id(0, dz, 0))
    gather(0, 2 * NZ, col_id(1, 0, 0))
    to_core(0)
    for dz in order:
        arrived(2 * dz)
        gather(2 * dz, 2 * NZ + 2 * dz, col_id(1, 0, 0))
        to_core(2 * dz)
    for dz in (0,) + order:
        arrived(2 * NZ + 2 * dz)
        to_core(2 * NZ + 2 * dz)
    for slot in range(1, 32, 2):
        arrived(slot)
    tok[...] = flat(xbuf[:, 0])
    grd[...] = flat(xbuf[:, 1])
    for load in loads:
        load.wait()

    def products(h):
        low, high = bounds[h]
        part = halves[h][0]
        part[:, 0] = jnp.dot(tok[...], wg[:, low:high], preferred_element_type=F32).reshape(32, 8, high - low)
        part[:, 1] = jnp.dot(tok[...], wu[:, low:high], preferred_element_type=F32).reshape(32, 8, high - low)
        part[:, 2] = lax.dot_general(
            grd[...], wd[low:high, :], LAST_DIMS, preferred_element_type=F32
        ).reshape(32, 8, high - low)

    def chain_in(h, side, k, t):
        _, _, in16, _, in32, _, _ = halves[h]
        return in16.at[side, k - 2, t] if narrow(side, k, t) else in32.at[side, k - 1, t]

    def chain(h, side, k, t, start=True):
        _, out16, _, out32, _, _, _ = halves[h]
        out = out16.at[side, k - 2, t] if narrow(side, k, t) else out32.at[side, k - 1, t]
        return remote(
            out, chain_in(h, side, k, t), c_send.at[h, side, k - 1, t], c_recv.at[h, side, k - 1, t],
            row_id(1 if side == 0 else NY - 1, 0), start,
        )

    def hop(h, k, near=True, distant=True):
        part, out16, _, out32, _, _, _ = halves[h]
        order = [(side, t) for t in range(NX) for side in (0, 1)]
        if k > 1:
            order = [p for p in order if not far(*p)] + [p for p in order if far(*p)]
        for side, t in order:
            if (k == 4 and not far(side, t)) or not (distant if far(side, t) else near):
                continue
            block = ((y + (k if side == 0 else NY - k)) % NY) * NX + (xh + 1 + t) % NX
            value = part[block]
            if k <= 2 or (k == 3 and far(side, t)):
                chain(h, side, k + 1, t, start=False).wait_recv()
                value += chain_in(h, side, k + 1, t)[...].astype(F32)
            if narrow(side, k, t):
                out16[side, k - 2, t] = value.astype(BF16)
            else:
                out32[side, k - 1, t] = value
            chain(h, side, k, t)

    def cross(h, t, there, start=True):
        _, _, _, out32, _, xin, _ = halves[h]
        return remote(
            xin.at[0, t], xin.at[1, t], x_send.at[h, t], x_recv.at[h, t], row_id(0, there), start
        )

    def turn(h):
        part, _, _, _, in32, xin, _ = halves[h]
        for t in range(NX):
            for side in (0, 1):
                chain(h, side, 1, t, start=False).wait_recv()
            xin[0, t] = in32[0, 0, t] + in32[1, 0, t] + part[y * NX + (xh + 1 + t) % NX]
            if t < NX - 1:
                cross(h, t, 1 + t)

    def share(h, t, block, start=True):
        hbuf = halves[h][6]
        return remote(
            hbuf.at[block], hbuf.at[block], h_send.at[h, t], h_recv.at[h, t], row_id(0, 1 + t), start
        )

    def forward(h, side, k, u, block, start=True):
        hbuf = halves[h][6]
        return remote(
            hbuf.at[block], hbuf.at[block], d_send.at[h, side, k - 1, u], d_recv.at[h, side, k - 1, u],
            row_id(1 if side == 0 else NY - 1, 0), start,
        )

    def source(side, k, u):
        return ((y + (NY - k if side == 0 else k)) % NY) * NX + (xh + NX - u) % NX

    def activate(h):
        _, _, _, _, _, xin, hbuf = halves[h]
        for t in (0, 2, 1):
            cross(h, t, 1 + t, start=False).wait_recv()
        sums = xin[0, NX - 1] + xin[1, 0] + xin[1, 1] + xin[1, 2]
        gate, upward, back = sums[0], sums[1], sums[2]
        sigma = jax.nn.sigmoid(gate)
        hbuf[mine, 0] = (gate * sigma * upward).astype(BF16)
        hbuf[mine, 1] = (back * upward * sigma * (1.0 + gate * (1.0 - sigma))).astype(BF16)
        hbuf[mine, 2] = (back * gate * sigma).astype(BF16)
        for side in (0, 1):
            forward(h, side, 1, 0, mine)
        for t in (0, 2, 1):
            share(h, t, mine)

    def spread(h, k):
        for u in (0, 1, 3, 2):
            if k == 1 and u == 0:
                continue
            if k == 1:
                share(h, u - 1, source(0, 0, u), start=False).wait_recv()
            for side in (0, 1):
                if k == 4 and not far(side, u):
                    continue
                block = source(side, k - 1, u)
                if k > 1:
                    forward(h, side, k - 1, u, block, start=False).wait_recv()
                forward(h, side, k, u, block)

    def landed(h):
        for u in (0, 1, 3, 2):
            for side in (0, 1):
                last = 4 if far(side, u) else 3
                forward(h, side, last, u, source(side, last, u), start=False).wait_recv()

    products(0)
    hop(0, 4)
    hop(0, 3, distant=False)
    products(1)
    hop(0, 3, near=False)
    hop(1, 4)
    hop(0, 2)
    hop(1, 3)
    hop(0, 1)
    hop(1, 2)
    turn(0)
    hop(1, 1)
    activate(0)
    turn(1)
    spread(0, 1)
    spread(0, 2)
    activate(1)
    spread(0, 3)
    spread(1, 1)
    spread(0, 4)
    spread(1, 2)
    spread(1, 3)
    spread(1, 4)
    landed(0)
    landed(1)

    def store(i):
        refs = ((gi_ref, gi_hbm), (gwg_ref, gwg_hbm), (gwu_ref, gwu_hbm), (gwd_ref, gwd_hbm))[i]
        copy = pltpu.make_async_copy(*refs, o_sem.at[i])
        copy.start()
        return copy

    grads = [(flat(half[6][:, 1]), flat(half[6][:, 2])) for half in halves]
    total = None
    for (low, high), (grad_gate, grad_up) in zip(bounds, grads):
        for grad, weight in ((grad_gate, wg), (grad_up, wu)):
            term = lax.dot_general(grad, weight[:, low:high], LAST_DIMS, preferred_element_type=F32)
            total = term if total is None else total + term
    total = total.reshape(16, 2, 8, total.shape[1])
    gpart[...] = total[:, 0]
    gcore[...] = total[:, 1]
    step = remote(gcore, gcore_in, e_send.at[8], e_recv.at[8], col_id(0, 0, 1))
    for (low, high), (grad_gate, _) in zip(bounds, grads):
        gwg_ref[:, low:high] = lax.dot_general(
            tok[...], grad_gate, FIRST_DIMS, preferred_element_type=F32
        ).astype(BF16)
    stored = [store(1)]
    step.wait_recv()
    gline[...] = gpart[NZ:] + gcore_in[NZ:]
    step = remote(gline, gline_in, e_send.at[9], e_recv.at[9], col_id(1, 0, 0))
    for (low, high), (_, grad_up) in zip(bounds, grads):
        gwu_ref[:, low:high] = lax.dot_general(
            tok[...], grad_up, FIRST_DIMS, preferred_element_type=F32
        ).astype(BF16)
    stored.append(store(2))
    step.wait_recv()
    gown[...] = gpart[:NZ] + gcore_in[:NZ] + gline_in[...]
    for dz in order:
        remote(gown.at[dz], gown_in.at[NZ - dz], e_send.at[NZ - dz], e_recv.at[NZ - dz], col_id(0, dz, 0))
    for (low, high), half in zip(bounds, halves):
        gwd_ref[low:high, :] = lax.dot_general(
            flat(half[6][:, 0]), grd[...], FIRST_DIMS, preferred_element_type=F32
        ).astype(BF16)
    stored.append(store(3))
    result = gown[0]
    for dz in order:
        remote(gown.at[dz], gown_in.at[dz], e_send.at[dz], e_recv.at[dz], col_id(0, dz, 0), start=False).wait_recv()
        result += gown_in[dz]
    gi_ref[...] = result.astype(BF16)
    stored.append(store(0))
    for copy in sent:
        copy.wait_send()
    for copy in stored:
        copy.wait()


def deliver(*refs):
    sources, targets, sems = refs[:4], refs[4:8], refs[8]
    copies = [pltpu.make_async_copy(s, t, sems.at[i]) for i, (s, t) in enumerate(zip(sources, targets))]
    for copy in copies:
        copy.start()
    for copy in copies:
        copy.wait()


def per_device(activations, out_grad, w_gate, w_up, w_down):
    depth, width = w_gate.shape
    cut = (width // 128 + 1) // 2 * 128
    bounds = ((0, cut), (cut, width))
    dma = pltpu.SemaphoreType.DMA
    hbm = pl.BlockSpec(memory_space=pltpu.MemorySpace.HBM)
    shapes = (
        jax.ShapeDtypeStruct((8, depth), BF16),
        jax.ShapeDtypeStruct((depth, width), BF16),
        jax.ShapeDtypeStruct((depth, width), BF16),
        jax.ShapeDtypeStruct((width, depth), BF16),
    )
    parts = []
    for low, high in bounds:
        block = (3, 8, high - low)
        parts += [
            pltpu.VMEM((32,) + block, F32),
            pltpu.VMEM((2, 3, NX) + block, BF16),
            pltpu.VMEM((2, 3, NX) + block, BF16),
            pltpu.VMEM((2, 2, NX) + block, F32),
            pltpu.VMEM((2, 2, NX) + block, F32),
            pltpu.VMEM((2, NX) + block, F32),
            pltpu.VMEM((32,) + block, BF16),
        ]
    n = len(bounds)
    results = pl.pallas_call(
        functools.partial(kernel, bounds),
        out_shape=shapes,
        in_specs=[hbm] * 5,
        out_specs=(hbm,) * 4,
        scratch_shapes=[pltpu.VMEM(shape.shape, BF16) for shape in shapes]
        + [
            pltpu.VMEM((depth, width), BF16),
            pltpu.VMEM((depth, width), BF16),
            pltpu.VMEM((width, depth), BF16),
            pltpu.VMEM((32, 2, 8, depth), BF16),
            pltpu.VMEM((256, depth), BF16),
            pltpu.VMEM((256, depth), BF16),
            pltpu.VMEM((16, 8, depth), F32),
            pltpu.VMEM((16, 8, depth), F32),
            pltpu.VMEM((16, 8, depth), F32),
            pltpu.VMEM((NZ, 8, depth), F32),
            pltpu.VMEM((NZ, 8, depth), F32),
            pltpu.VMEM((NZ, 8, depth), F32),
            pltpu.VMEM((NZ, 8, depth), F32),
            dma((5,)), dma((4,)),
            dma((32,)), dma((32,)),
            dma((n, 2, 4, NX)), dma((n, 2, 4, NX)),
            dma((n, NX - 1)), dma((n, NX - 1)),
            dma((n, NX - 1)), dma((n, NX - 1)),
            dma((n, 2, 4, NX)), dma((n, 2, 4, NX)),
            dma((10,)), dma((10,)),
        ] + parts,
        compiler_params=pltpu.CompilerParams(collective_id=0, has_side_effects=True, vmem_limit_bytes=60 << 20),
        name="ffn_backward",
    )(activations, out_grad, w_gate, w_up, w_down)
    return pl.pallas_call(
        deliver,
        out_shape=shapes,
        in_specs=[hbm] * 4,
        out_specs=(hbm,) * 4,
        scratch_shapes=[dma((4,))],
        name="deliver",
    )(*results)


def solution(mesh):
    in_specs = (P("col", "row"), P("col", "row"), P("row", "col"), P("row", "col"), P("col", "row"))
    out_specs = (P("col", "row"), P("row", "col"), P("row", "col"), P("col", "row"))
    return jax.shard_map(
        per_device, mesh=mesh, in_specs=in_specs, out_specs=out_specs, check_vma=False
    )
```

time: 715 us -> 137 us (0.19)
  waiting for transfers between devices: 408 us -> 0 us
  blocking collectives: 277 us -> 0 us
  Pallas kernels: 0 us -> 136 us
  between operations: 14.8 us -> 0.64 us
    unnamed x3 -> x0, waiting for transfers between devices: 312 us -> none
    all_gather x5 -> x0, blocking collectives: 277 us -> none  [the longest x1 66.9 us: per_device(): lax.all_gather(up_part, 'row', axis=0, tiled=True)]
    pallas_call x0 -> x2, Pallas kernels: none -> 136 us  [the longest x1 93 us: per_device(): pl.pallas_call(functools.partial(kernel, bounds), out_shape=shapes, in_sp...]
    reduce_scatter x1 -> x0, waiting for transfers between devices: 95.5 us -> none  [per_device(): lax.psum_scatter(result + lax.dot_general(grad_up, w_up, contract_last, p...]
  transfers between devices with their start and end apart: 2 -> 0, of which waited for: 2 -> 0; matrix products, arithmetic and copies ran while one was open for 1% -> 0% of each run, Pallas kernels for 0% -> 0%
where the time goes in v2:
time: 137 us
  Pallas kernels  136 us (99%)
    pallas_call x1, Pallas kernels, per_device(): pl.pallas_call(functools.partial(kernel, bounds), out_shape=shapes, in_sp...  93 us
    pallas_call x1, Pallas kernels, per_device(): pl.pallas_call(deliver, out_shape=shapes, in_specs=[hbm] * 4, out_specs=(...  43 us

profile of v2, /device:TPU:1, one launch (start us, length us, event | category | flops | bytes accessed | tf_op | source)
XLA Modules:
  0.0 136.6 jit_solution(46903347899527500)
XLA Ops:
  0.6 93.0 %ffn_backward.1 = (bf16[8,256]{1,0:T(8,128)(2,1)}, bf16[256,896]{1,0:T(8,128)(2,1)}, bf16[256,896]{1,0:T(8,128)(2,1)}, bf16[896,256]{1,0:T(8,128)(2,1)}) custom-call(bf16[8,256]{1,0:T(8,128)(2,1)} %act_hbm.1, bf16[8,256]{1,0:T(8,128)(2,1)} %og_hbm.1, bf16[256,896]{1,0:T(8,128)(2,1)} %wg_hbm.1, bf16[256,896]{1,0:T(8,128)(2,1)} %wu_hbm.1, bf16[896,256]{1,0:T(8,128)(2,1)} %wd_hbm.1), custom_call_target="tpu_custom_call" | custom-call | tf_op jit(solution)/shard_map/ffn_backward/pallas_call | solution.py:327
  93.7 43.0 %deliver.1 = (bf16[8,256]{1,0:T(8,128)(2,1)}, bf16[256,896]{1,0:T(8,128)(2,1)}, bf16[256,896]{1,0:T(8,128)(2,1)}, bf16[896,256]{1,0:T(8,128)(2,1)}) custom-call(bf16[8,256]{1,0:T(8,128)(2,1)} %get-tuple-element.8.refs_0_, bf16[256,896]{1,0:T(8,128)(2,1)} %get-tuple-element.9.refs_1_, bf16[256,896]{1,0:T(8,128)(2,1)} %get-tuple-element.10.refs_2_, ...), custom_call_target="tpu_custom_call" | custom-call | tf_op jit(solution)/shard_map/deliver/pallas_call | solution.py:358

commit v3 on v2

--- a/solution.py
+++ b/solution.py
@@ -32,9 +32,9 @@
 def kernel(
     bounds,
     act_hbm, og_hbm, wg_hbm, wu_hbm, wd_hbm,
-    gi_hbm, gwg_hbm, gwu_hbm, gwd_hbm,
-    gi_ref, gwg_ref, gwu_ref, gwd_ref, wg, wu, wd, xbuf, tok, grd, gpart, gcore, gcore_in, gline, gline_in, gown, gown_in,
-    w_sem, o_sem, a_send, a_recv, c_send, c_recv, x_send, x_recv, h_send, h_recv, d_send, d_recv, e_send, e_recv,
+    gi_ref, gwg_ref, gwu_ref, gwd_ref,
+    wg, wu, wd, xbuf, tok, grd, gpart, gsend, grecv,
+    w_sem, a_send, a_recv, c_send, c_recv, x_send, x_recv, h_send, h_recv, d_send, d_recv, e_send, e_recv,
     *parts,
 ):
     row, col = lax.axis_index("row"), lax.axis_index("col")
@@ -45,6 +45,12 @@
 
     def col_id(dx, dz, dc):
         return (row, ((xl + dx) % 2) * (2 * NZ) + ((z + dz) % NZ) * 2 + (core + dc) % 2)
+
+    def slot_id(slot):
+        return col_id(slot // (2 * NZ), (slot // 2) % NZ, slot % 2)
+
+    def slot_there(slot):
+        return slot // (2 * NZ) * (2 * NZ) + (NZ - (slot // 2) % NZ) % NZ * 2 + slot % 2
 
     def row_id(dy, dx):
         return (((y + dy) % NY) * NX + (xh + dx) % NX, col)
@@ -72,37 +78,31 @@
         load.start()
 
     barrier = pltpu.get_barrier_semaphore()
-    partners = [col_id(0, dz, 0) for dz in range(1, NZ)] + [col_id(1, 0, 0), col_id(0, 0, 1)]
-    partners += [row_id(1, 0), row_id(NY - 1, 0)] + [row_id(0, dx) for dx in range(1, NX)]
+
+    def greet(slot, carry):
+        pl.semaphore_signal(barrier, inc=1, device_id=slot_id(slot), device_id_type=MESH)
+        return carry
+
+    lax.fori_loop(1, 32, greet, 0)
+    partners = [row_id(1, 0), row_id(NY - 1, 0)] + [row_id(0, dx) for dx in range(1, NX)]
     for partner in partners:
         pl.semaphore_signal(barrier, inc=1, device_id=partner, device_id_type=MESH)
     for load in own:
         load.wait()
-    pl.semaphore_wait(barrier, len(partners))
+    pl.semaphore_wait(barrier, 31 + len(partners))
 
     def gather(slot, there, device, start=True):
         return remote(xbuf.at[slot], xbuf.at[there], a_send.at[there], a_recv.at[there], device, start)
 
-    def arrived(slot):
-        gather(slot, slot, col_id(0, 0, 1), start=False).wait_recv()
-
-    def to_core(slot):
-        gather(slot, slot + 1, col_id(0, 0, 1))
-
-    order = (1, 7, 2, 6, 3, 5, 4)
-    for dz in order:
-        gather(0, (NZ - dz) * 2, col_id(0, dz, 0))
-    gather(0, 2 * NZ, col_id(1, 0, 0))
-    to_core(0)
-    for dz in order:
-        arrived(2 * dz)
-        gather(2 * dz, 2 * NZ + 2 * dz, col_id(1, 0, 0))
-        to_core(2 * dz)
-    for dz in (0,) + order:
-        arrived(2 * NZ + 2 * dz)
-        to_core(2 * NZ + 2 * dz)
-    for slot in range(1, 32, 2):
-        arrived(slot)
+    order = [dx * 2 * NZ + dz * 2 for dz in (0, 1, 7, 2, 6, 3, 5, 4) for dx in (0, 1)]
+    for slot in order[1:]:
+        gather(0, slot_there(slot), slot_id(slot))
+    for slot in order:
+        if slot > 0:
+            gather(slot, slot, slot_id(1), start=False).wait_recv()
+        gather(slot, slot + 1, slot_id(1))
+    for slot in order:
+        gather(slot + 1, slot + 1, slot_id(1), start=False).wait_recv()
     tok[...] = flat(xbuf[:, 0])
     grd[...] = flat(xbuf[:, 1])
     for load in loads:
@@ -240,54 +240,43 @@
     landed(0)
     landed(1)
 
-    def store(i):
-        refs = ((gi_ref, gi_hbm), (gwg_ref, gwg_hbm), (gwu_ref, gwu_hbm), (gwd_ref, gwd_hbm))[i]
-        copy = pltpu.make_async_copy(*refs, o_sem.at[i])
-        copy.start()
-        return copy
-
     grads = [(flat(half[6][:, 1]), flat(half[6][:, 2])) for half in halves]
     total = None
     for (low, high), (grad_gate, grad_up) in zip(bounds, grads):
         for grad, weight in ((grad_gate, wg), (grad_up, wu)):
             term = lax.dot_general(grad, weight[:, low:high], LAST_DIMS, preferred_element_type=F32)
             total = term if total is None else total + term
-    total = total.reshape(16, 2, 8, total.shape[1])
-    gpart[...] = total[:, 0]
-    gcore[...] = total[:, 1]
-    step = remote(gcore, gcore_in, e_send.at[8], e_recv.at[8], col_id(0, 0, 1))
-    for (low, high), (grad_gate, _) in zip(bounds, grads):
-        gwg_ref[:, low:high] = lax.dot_general(
-            tok[...], grad_gate, FIRST_DIMS, preferred_element_type=F32
-        ).astype(BF16)
-    stored = [store(1)]
-    step.wait_recv()
-    gline[...] = gpart[NZ:] + gcore_in[NZ:]
-    step = remote(gline, gline_in, e_send.at[9], e_recv.at[9], col_id(1, 0, 0))
-    for (low, high), (_, grad_up) in zip(bounds, grads):
-        gwu_ref[:, low:high] = lax.dot_general(
-            tok[...], grad_up, FIRST_DIMS, preferred_element_type=F32
-        ).astype(BF16)
-    stored.append(store(2))
-    step.wait_recv()
-    gown[...] = gpart[:NZ] + gcore_in[:NZ] + gline_in[...]
-    for dz in order:
-        remote(gown.at[dz], gown_in.at[NZ - dz], e_send.at[NZ - dz], e_recv.at[NZ - dz], col_id(0, dz, 0))
-    for (low, high), half in zip(bounds, halves):
+    gpart[...] = total.reshape(32, 8, total.shape[1])
+    gsend[...] = gpart[...].astype(BF16)
+
+    def returned(slot, there, device):
+        return pltpu.make_async_remote_copy(
+            src_ref=gsend.at[slot], dst_ref=grecv.at[there], send_sem=e_send.at[slot], recv_sem=e_recv.at[there],
+            device_id=device, device_id_type=MESH,
+        )
+
+    def return_start(slot, carry):
+        returned(slot, slot_there(slot), slot_id(slot)).start()
+        return carry
+
+    lax.fori_loop(1, 32, return_start, 0)
+    for (low, high), half, (grad_gate, grad_up) in zip(bounds, halves, grads):
+        for out, grad in ((gwg_ref, grad_gate), (gwu_ref, grad_up)):
+            out[:, low:high] = lax.dot_general(
+                tok[...], grad, FIRST_DIMS, preferred_element_type=F32
+            ).astype(BF16)
         gwd_ref[low:high, :] = lax.dot_general(
             flat(half[6][:, 0]), grd[...], FIRST_DIMS, preferred_element_type=F32
         ).astype(BF16)
-    stored.append(store(3))
-    result = gown[0]
-    for dz in order:
-        remote(gown.at[dz], gown_in.at[dz], e_send.at[dz], e_recv.at[dz], col_id(0, dz, 0), start=False).wait_recv()
-        result += gown_in[dz]
-    gi_ref[...] = result.astype(BF16)
-    stored.append(store(0))
     for copy in sent:
         copy.wait_send()
-    for copy in stored:
-        copy.wait()
+
+    def return_wait(slot, carry):
+        returned(slot, slot, slot_id(slot)).wait()
+        return carry
+
+    lax.fori_loop(1, 32, return_wait, 0)
+    gi_ref[...] = (gpart[0] + jnp.sum(grecv[1:].astype(F32), axis=0)).astype(BF16)
 
 
 def deliver(*refs):
@@ -304,6 +293,7 @@
     cut = (width // 128 + 1) // 2 * 128
     bounds = ((0, cut), (cut, width))
     dma = pltpu.SemaphoreType.DMA
+    vmem = pl.BlockSpec(memory_space=pltpu.VMEM)
     hbm = pl.BlockSpec(memory_space=pltpu.MemorySpace.HBM)
     shapes = (
         jax.ShapeDtypeStruct((8, depth), BF16),
@@ -324,43 +314,40 @@
             pltpu.VMEM((32,) + block, BF16),
         ]
     n = len(bounds)
+    operands = [pltpu.with_memory_space_constraint(x, pltpu.MemorySpace.HBM) for x in (activations, out_grad, w_gate, w_up, w_down)]
     results = pl.pallas_call(
         functools.partial(kernel, bounds),
-        out_shape=shapes,
+        out_shape=tuple(pltpu.VMEM(shape.shape, BF16) for shape in shapes),
         in_specs=[hbm] * 5,
-        out_specs=(hbm,) * 4,
-        scratch_shapes=[pltpu.VMEM(shape.shape, BF16) for shape in shapes]
-        + [
+        out_specs=(vmem,) * 4,
+        scratch_shapes=[
             pltpu.VMEM((depth, width), BF16),
             pltpu.VMEM((depth, width), BF16),
             pltpu.VMEM((width, depth), BF16),
             pltpu.VMEM((32, 2, 8, depth), BF16),
             pltpu.VMEM((256, depth), BF16),
             pltpu.VMEM((256, depth), BF16),
-            pltpu.VMEM((16, 8, depth), F32),
-            pltpu.VMEM((16, 8, depth), F32),
-            pltpu.VMEM((16, 8, depth), F32),
-            pltpu.VMEM((NZ, 8, depth), F32),
-            pltpu.VMEM((NZ, 8, depth), F32),
-            pltpu.VMEM((NZ, 8, depth), F32),
-            pltpu.VMEM((NZ, 8, depth), F32),
-            dma((5,)), dma((4,)),
+            pltpu.VMEM((32, 8, depth), F32),
+            pltpu.VMEM((32, 8, depth), BF16),
+            pltpu.VMEM((32, 8, depth), BF16),
+            dma((5,)),
             dma((32,)), dma((32,)),
             dma((n, 2, 4, NX)), dma((n, 2, 4, NX)),
             dma((n, NX - 1)), dma((n, NX - 1)),
             dma((n, NX - 1)), dma((n, NX - 1)),
             dma((n, 2, 4, NX)), dma((n, 2, 4, NX)),
-            dma((10,)), dma((10,)),
+            dma((32,)), dma((32,)),
         ] + parts,
         compiler_params=pltpu.CompilerParams(collective_id=0, has_side_effects=True, vmem_limit_bytes=60 << 20),
         name="ffn_backward",
-    )(activations, out_grad, w_gate, w_up, w_down)
+    )(*operands)
     return pl.pallas_call(
         deliver,
         out_shape=shapes,
-        in_specs=[hbm] * 4,
+        in_specs=[vmem] * 4,
         out_specs=(hbm,) * 4,
         scratch_shapes=[dma((4,))],
+        compiler_params=pltpu.CompilerParams(vmem_limit_bytes=4 << 20),
         name="deliver",
     )(*results)
 

time: 137 us -> 92.6 us (0.68)
  Pallas kernels: 136 us -> 91.8 us
    pallas_call x2, Pallas kernels: 136 us -> 91.8 us  [the longest x1 90.7 us: per_device(): pl.pallas_call(functools.partial(kernel, bounds), out_shape=tuple((pltpu....]
where the time goes in v3:
time: 92.6 us; the launch traced here: 92.5 us
  Pallas kernels  91.8 us (99%)
    pallas_call x1, Pallas kernels, per_device(): pl.pallas_call(functools.partial(kernel, bounds), out_shape=tuple((pltpu....  90.7 us

profile of v3, /device:TPU:1, one launch (start us, length us, event | category | flops | bytes accessed | tf_op | source)
XLA Modules:
  0.0 92.5 jit_solution(11141531797163661951)
XLA Ops:
  0.6 90.7 %ffn_backward.1 = (bf16[8,256]{1,0:T(8,128)(2,1)S(1)}, bf16[256,896]{1,0:T(8,128)(2,1)S(1)}, bf16[256,896]{1,0:T(8,128)(2,1)S(1)}, bf16[896,256]{1,0:T(8,128)(2,1)S(1)}) custom-call(bf16[8,256]{1,0:T(8,128)(2,1)} %act_hbm.1, bf16[8,256]{1,0:T(8,128)(2,1)} %og_hbm.1, bf16[256,896]{1,0:T(8,128)(2,1)} %wg_hbm.1, bf16[256,896]{1,0:T(8,128)(2,1)} %wu_hbm.1, ...), custom_call_target="tpu_custom_call" | custom-call | tf_op jit(solution)/shard_map/ffn_backward/pallas_call | solution.py:318
  91.3 1.1 %deliver.1 = (bf16[8,256]{1,0:T(8,128)(2,1)}, bf16[256,896]{1,0:T(8,128)(2,1)}, bf16[256,896]{1,0:T(8,128)(2,1)}, bf16[896,256]{1,0:T(8,128)(2,1)}) custom-call(bf16[8,256]{1,0:T(8,128)(2,1)S(1)} %get-tuple-element.8.refs_0_, bf16[256,896]{1,0:T(8,128)(2,1)S(1)} %get-tuple-element.9.refs_1_, bf16[256,896]{1,0:T(8,128)(2,1)S(1)} %get-tuple-element.10.refs_2_, ...), custom_call_target="tpu_custom_call" | custom-call | tf_op jit(solution)/shard_map/deliver/pallas_call | solution.py:344

commit v4 on v3

--- a/solution.py
+++ b/solution.py
@@ -12,8 +12,38 @@
 BF16 = jnp.bfloat16
 
 NY, NX, NZ = 8, 4, 8
+FIRST, LATER = (4, 3, 5), (2, 6, 1, 7, 0)
 LAST_DIMS = (((1,), (1,)), ((), ()))
 FIRST_DIMS = (((0,), (0,)), ((), ()))
+
+
+ORDER = (
+    (0, 1, 4, 0, 0), (0, 1, 4, 0, 1), (0, 1, 4, 1, 2), (0, 1, 4, 1, 3), (0, 1, 3, 0, 2), (0, 1, 3, 0, 3),
+    (0, 1, 3, 1, 0), (0, 1, 3, 1, 1), (0, 0, 4, 0, 0), (0, 0, 4, 0, 1), (0, 0, 4, 1, 2), (0, 0, 4, 1, 3),
+    (0, 0, 3, 0, 2), (0, 0, 3, 0, 3), (0, 1, 3, 0, 0), (0, 1, 3, 0, 1), (0, 1, 3, 1, 2), (0, 1, 3, 1, 3),
+    (0, 0, 3, 1, 0), (0, 0, 3, 1, 1), (0, 2, 4, 0, 0), (0, 2, 4, 0, 1), (0, 0, 3, 0, 0), (4, 0), (0, 1, 2, 0, 2),
+    (0, 1, 2, 0, 3), (0, 1, 2, 1, 0), (0, 1, 2, 1, 1), (0, 1, 2, 1, 2), (0, 1, 2, 0, 0), (0, 1, 2, 1, 3),
+    (0, 1, 2, 0, 1), (0, 0, 3, 1, 2), (0, 0, 3, 0, 1), (0, 0, 3, 1, 3), (0, 2, 4, 1, 2), (0, 2, 4, 1, 3),
+    (0, 0, 2, 0, 2), (0, 1, 1, 0, 2), (0, 1, 1, 0, 3), (0, 1, 1, 1, 0), (0, 1, 1, 1, 1), (0, 0, 2, 0, 3),
+    (0, 0, 2, 1, 0), (0, 1, 1, 0, 0), (0, 1, 1, 1, 2), (0, 0, 2, 1, 1), (0, 1, 1, 0, 1), (0, 1, 1, 1, 3),
+    (0, 0, 2, 0, 0), (0, 0, 2, 0, 1), (0, 0, 2, 1, 2), (0, 0, 2, 1, 3), (0, 2, 3, 0, 2), (0, 2, 3, 0, 3),
+    (0, 2, 3, 1, 0), (0, 2, 3, 1, 1), (0, 2, 3, 0, 0), (0, 2, 3, 0, 1), (0, 2, 3, 1, 2), (0, 2, 3, 1, 3),
+    (0, 0, 1, 0, 2), (0, 0, 1, 0, 3), (1, 1, 0), (0, 0, 1, 1, 0), (1, 1, 1), (1, 1, 2), (0, 0, 1, 1, 1),
+    (0, 0, 1, 0, 0), (1, 1, 3), (0, 0, 1, 0, 1), (0, 0, 1, 1, 2), (0, 2, 2, 0, 2), (0, 2, 2, 0, 3), (0, 2, 2, 0, 0),
+    (0, 0, 1, 1, 3), (0, 2, 2, 0, 1), (0, 2, 2, 1, 0), (0, 2, 2, 1, 1), (0, 2, 2, 1, 2), (0, 2, 2, 1, 3), (2, 1),
+    (1, 0, 0), (1, 0, 1), (1, 0, 2), (0, 2, 1, 0, 2), (0, 2, 1, 0, 3), (1, 0, 3), (0, 2, 1, 0, 0), (0, 2, 1, 1, 0),
+    (0, 2, 1, 1, 1), (0, 2, 1, 0, 1), (3, 1, 2, 0, 0), (0, 2, 1, 1, 2), (3, 1, 2, 0, 1), (3, 1, 2, 0, 3),
+    (0, 2, 1, 1, 3), (3, 1, 2, 0, 2), (3, 1, 2, 1, 0), (3, 1, 2, 1, 1), (3, 1, 2, 1, 3), (3, 1, 2, 1, 2), (1, 2, 0),
+    (1, 2, 1), (3, 1, 3, 0, 0), (1, 2, 2), (3, 1, 3, 0, 1), (2, 0), (3, 1, 3, 0, 3), (3, 1, 3, 0, 2), (3, 1, 3, 1, 0),
+    (3, 1, 3, 1, 1), (3, 1, 3, 1, 3), (1, 2, 3), (3, 1, 3, 1, 2), (3, 1, 4, 0, 0), (3, 1, 4, 0, 1), (3, 0, 2, 0, 0),
+    (3, 0, 2, 1, 0), (3, 0, 2, 0, 1), (3, 0, 2, 1, 1), (2, 2), (3, 0, 2, 0, 3), (3, 0, 2, 1, 3), (3, 0, 2, 0, 2),
+    (3, 0, 2, 1, 2), (3, 1, 4, 1, 3), (3, 1, 4, 1, 2), (3, 0, 3, 0, 0), (3, 0, 3, 1, 0), (3, 0, 3, 0, 1),
+    (3, 0, 3, 1, 1), (3, 2, 2, 0, 0), (3, 2, 2, 1, 0), (3, 2, 2, 0, 1), (3, 2, 2, 1, 1), (3, 2, 2, 0, 3),
+    (3, 2, 2, 1, 3), (3, 2, 2, 0, 2), (3, 2, 2, 1, 2), (3, 0, 3, 0, 3), (3, 0, 3, 1, 3), (3, 0, 3, 0, 2),
+    (3, 0, 3, 1, 2), (3, 0, 4, 0, 0), (3, 0, 4, 0, 1), (3, 2, 3, 0, 0), (3, 2, 3, 0, 1), (3, 2, 3, 1, 0),
+    (3, 2, 3, 0, 3), (3, 2, 3, 1, 1), (3, 2, 3, 0, 2), (3, 2, 3, 1, 3), (3, 2, 3, 1, 2), (5, 0), (3, 0, 4, 1, 3),
+    (3, 0, 4, 1, 2), (3, 2, 4, 0, 0), (3, 2, 4, 0, 1), (3, 2, 4, 1, 3), (3, 2, 4, 1, 2),
+)
 
 
 def flat(value):
@@ -84,38 +114,54 @@
         return carry
 
     lax.fori_loop(1, 32, greet, 0)
-    partners = [row_id(1, 0), row_id(NY - 1, 0)] + [row_id(0, dx) for dx in range(1, NX)]
+    partners = [row_id(dy, dx) for dy in (0, 1, NY - 1) for dx in range(NX) if dy or dx]
     for partner in partners:
         pl.semaphore_signal(barrier, inc=1, device_id=partner, device_id_type=MESH)
     for load in own:
         load.wait()
     pl.semaphore_wait(barrier, 31 + len(partners))
 
-    def gather(slot, there, device, start=True):
-        return remote(xbuf.at[slot], xbuf.at[there], a_send.at[there], a_recv.at[there], device, start)
-
-    order = [dx * 2 * NZ + dz * 2 for dz in (0, 1, 7, 2, 6, 3, 5, 4) for dx in (0, 1)]
-    for slot in order[1:]:
-        gather(0, slot_there(slot), slot_id(slot))
-    for slot in order:
-        if slot > 0:
-            gather(slot, slot, slot_id(1), start=False).wait_recv()
-        gather(slot, slot + 1, slot_id(1))
-    for slot in order:
-        gather(slot + 1, slot + 1, slot_id(1), start=False).wait_recv()
-    tok[...] = flat(xbuf[:, 0])
-    grd[...] = flat(xbuf[:, 1])
+    def blocks(steps, visit, skip_own=True):
+        def body(i, carry):
+            step = sum(((i // NX == n) * d for n, d in enumerate(steps)), 0)
+            slot = (y + step) % NY * NX + i % NX
+
+            @pl.when(slot != 0)
+            def _():
+                visit(slot)
+
+            return carry
+
+        lax.fori_loop(0, len(steps) * NX, body, 0)
+
+    def gather(slot, there):
+        return pltpu.make_async_remote_copy(
+            src_ref=xbuf.at[0], dst_ref=xbuf.at[there], send_sem=a_send.at[there], recv_sem=a_recv.at[there],
+            device_id=slot_id(slot), device_id_type=MESH,
+        )
+
+    def rows(step):
+        return pl.ds((y + step) % NY * NX, NX)
+
+    def stack(values):
+        return jnp.concatenate([v.astype(F32).reshape(32, v.shape[2]) for v in values], axis=0).astype(BF16)
+
+    def products(steps):
+        blocks(steps, lambda slot: gather(slot, slot).wait_recv())
+        here = [xbuf[rows(step)] for step in steps]
+        tokens, grads = stack([v[:, 0] for v in here]), stack([v[:, 1] for v in here])
+        for (low, high), half in zip(bounds, halves):
+            gate = jnp.dot(tokens, wg[:, low:high], preferred_element_type=F32)
+            upward = jnp.dot(tokens, wu[:, low:high], preferred_element_type=F32)
+            back = lax.dot_general(grads, wd[low:high, :], LAST_DIMS, preferred_element_type=F32)
+            for q, value in enumerate((gate, upward, back)):
+                for n, step in enumerate(steps):
+                    half[0][rows(step), q] = value[32 * n : 32 * n + 32].reshape(NX, 8, high - low)
+
+    blocks(FIRST + LATER, lambda slot: gather(slot_there(slot), slot).start())
     for load in loads:
         load.wait()
-
-    def products(h):
-        low, high = bounds[h]
-        part = halves[h][0]
-        part[:, 0] = jnp.dot(tok[...], wg[:, low:high], preferred_element_type=F32).reshape(32, 8, high - low)
-        part[:, 1] = jnp.dot(tok[...], wu[:, low:high], preferred_element_type=F32).reshape(32, 8, high - low)
-        part[:, 2] = lax.dot_general(
-            grd[...], wd[low:high, :], LAST_DIMS, preferred_element_type=F32
-        ).reshape(32, 8, high - low)
+    products(FIRST)
 
     def chain_in(h, side, k, t):
         _, _, in16, _, in32, _, _ = halves[h]
@@ -129,24 +175,17 @@
             row_id(1 if side == 0 else NY - 1, 0), start,
         )
 
-    def hop(h, k, near=True, distant=True):
+    def hop(h, k, side, t):
         part, out16, _, out32, _, _, _ = halves[h]
-        order = [(side, t) for t in range(NX) for side in (0, 1)]
-        if k > 1:
-            order = [p for p in order if not far(*p)] + [p for p in order if far(*p)]
-        for side, t in order:
-            if (k == 4 and not far(side, t)) or not (distant if far(side, t) else near):
-                continue
-            block = ((y + (k if side == 0 else NY - k)) % NY) * NX + (xh + 1 + t) % NX
-            value = part[block]
-            if k <= 2 or (k == 3 and far(side, t)):
-                chain(h, side, k + 1, t, start=False).wait_recv()
-                value += chain_in(h, side, k + 1, t)[...].astype(F32)
-            if narrow(side, k, t):
-                out16[side, k - 2, t] = value.astype(BF16)
-            else:
-                out32[side, k - 1, t] = value
-            chain(h, side, k, t)
+        value = part[((y + (k if side == 0 else NY - k)) % NY) * NX + (xh + 1 + t) % NX]
+        if k <= 2 or (k == 3 and far(side, t)):
+            chain(h, side, k + 1, t, start=False).wait_recv()
+            value += chain_in(h, side, k + 1, t)[...].astype(F32)
+        if narrow(side, k, t):
+            out16[side, k - 2, t] = value.astype(BF16)
+        else:
+            out32[side, k - 1, t] = value
+        chain(h, side, k, t)
 
     def cross(h, t, there, start=True):
         _, _, _, out32, _, xin, _ = halves[h]
@@ -154,14 +193,13 @@
             xin.at[0, t], xin.at[1, t], x_send.at[h, t], x_recv.at[h, t], row_id(0, there), start
         )
 
-    def turn(h):
+    def turn(h, t):
         part, _, _, _, in32, xin, _ = halves[h]
-        for t in range(NX):
-            for side in (0, 1):
-                chain(h, side, 1, t, start=False).wait_recv()
-            xin[0, t] = in32[0, 0, t] + in32[1, 0, t] + part[y * NX + (xh + 1 + t) % NX]
-            if t < NX - 1:
-                cross(h, t, 1 + t)
+        for side in (0, 1):
+            chain(h, side, 1, t, start=False).wait_recv()
+        xin[0, t] = in32[0, 0, t] + in32[1, 0, t] + part[y * NX + (xh + 1 + t) % NX]
+        if t < NX - 1:
+            cross(h, t, 1 + t)
 
     def share(h, t, block, start=True):
         hbuf = halves[h][6]
@@ -173,7 +211,7 @@
         hbuf = halves[h][6]
         return remote(
             hbuf.at[block], hbuf.at[block], d_send.at[h, side, k - 1, u], d_recv.at[h, side, k - 1, u],
-            row_id(1 if side == 0 else NY - 1, 0), start,
+            row_id(1 if side == 0 else NY - 1, u if k == 1 else 0), start,
         )
 
     def source(side, k, u):
@@ -193,77 +231,58 @@
             forward(h, side, 1, 0, mine)
         for t in (0, 2, 1):
             share(h, t, mine)
-
-    def spread(h, k):
-        for u in (0, 1, 3, 2):
-            if k == 1 and u == 0:
-                continue
-            if k == 1:
-                share(h, u - 1, source(0, 0, u), start=False).wait_recv()
+        for u in (1, 3, 2):
             for side in (0, 1):
-                if k == 4 and not far(side, u):
-                    continue
-                block = source(side, k - 1, u)
-                if k > 1:
-                    forward(h, side, k - 1, u, block, start=False).wait_recv()
-                forward(h, side, k, u, block)
-
-    def landed(h):
+                forward(h, side, 1, u, mine)
+
+    def spread(h, k, side, u):
+        block = source(side, k - 1, u)
+        forward(h, side, k - 1, u, block, start=False).wait_recv()
+        forward(h, side, k, u, block)
+
+    def returned(slot, there):
+        return pltpu.make_async_remote_copy(
+            src_ref=gsend.at[slot], dst_ref=grecv.at[there], send_sem=e_send.at[slot], recv_sem=e_recv.at[there],
+            device_id=slot_id(slot), device_id_type=MESH,
+        )
+
+    def give_back(steps):
+        total = None
+        for (low, high), half in zip(bounds, halves):
+            here = [half[6][rows(step)] for step in steps]
+            for q, weight in ((1, wg), (2, wu)):
+                term = lax.dot_general(
+                    stack([v[:, q] for v in here]), weight[:, low:high], LAST_DIMS, preferred_element_type=F32
+                )
+                total = term if total is None else total + term
+        for n, step in enumerate(steps):
+            value = total[32 * n : 32 * n + 32].reshape(NX, 8, total.shape[1])
+            gpart[rows(step)] = value
+            gsend[rows(step)] = value.astype(BF16)
+        blocks(steps, lambda slot: returned(slot, slot_there(slot)).start())
+
+    def nearer():
+        for h in range(len(bounds)):
+            for t in range(NX - 1):
+                share(h, t, source(0, 0, t + 1), start=False).wait_recv()
+        give_back(LATER)
+
+    steps = (hop, turn, activate, spread, lambda _: products(LATER), lambda _: nearer())
+    for kind, *where in ORDER:
+        steps[kind](*where)
+    for h in range(len(bounds)):
         for u in (0, 1, 3, 2):
             for side in (0, 1):
                 last = 4 if far(side, u) else 3
                 forward(h, side, last, u, source(side, last, u), start=False).wait_recv()
-
-    products(0)
-    hop(0, 4)
-    hop(0, 3, distant=False)
-    products(1)
-    hop(0, 3, near=False)
-    hop(1, 4)
-    hop(0, 2)
-    hop(1, 3)
-    hop(0, 1)
-    hop(1, 2)
-    turn(0)
-    hop(1, 1)
-    activate(0)
-    turn(1)
-    spread(0, 1)
-    spread(0, 2)
-    activate(1)
-    spread(0, 3)
-    spread(1, 1)
-    spread(0, 4)
-    spread(1, 2)
-    spread(1, 3)
-    spread(1, 4)
-    landed(0)
-    landed(1)
-
-    grads = [(flat(half[6][:, 1]), flat(half[6][:, 2])) for half in halves]
-    total = None
-    for (low, high), (grad_gate, grad_up) in zip(bounds, grads):
-        for grad, weight in ((grad_gate, wg), (grad_up, wu)):
-            term = lax.dot_general(grad, weight[:, low:high], LAST_DIMS, preferred_element_type=F32)
-            total = term if total is None else total + term
-    gpart[...] = total.reshape(32, 8, total.shape[1])
-    gsend[...] = gpart[...].astype(BF16)
-
-    def returned(slot, there, device):
-        return pltpu.make_async_remote_copy(
-            src_ref=gsend.at[slot], dst_ref=grecv.at[there], send_sem=e_send.at[slot], recv_sem=e_recv.at[there],
-            device_id=device, device_id_type=MESH,
-        )
-
-    def return_start(slot, carry):
-        returned(slot, slot_there(slot), slot_id(slot)).start()
-        return carry
-
-    lax.fori_loop(1, 32, return_start, 0)
-    for (low, high), half, (grad_gate, grad_up) in zip(bounds, halves, grads):
-        for out, grad in ((gwg_ref, grad_gate), (gwu_ref, grad_up)):
+    give_back(FIRST)
+
+    tok[...] = flat(xbuf[:, 0])
+    grd[...] = flat(xbuf[:, 1])
+    for (low, high), half in zip(bounds, halves):
+        for out, q in ((gwg_ref, 1), (gwu_ref, 2)):
             out[:, low:high] = lax.dot_general(
-                tok[...], grad, FIRST_DIMS, preferred_element_type=F32
+                tok[...], flat(half[6][:, q]), FIRST_DIMS, preferred_element_type=F32
             ).astype(BF16)
         gwd_ref[low:high, :] = lax.dot_general(
             flat(half[6][:, 0]), grd[...], FIRST_DIMS, preferred_element_type=F32
@@ -271,11 +290,12 @@
     for copy in sent:
         copy.wait_send()
 
-    def return_wait(slot, carry):
-        returned(slot, slot, slot_id(slot)).wait()
+    def finish(slot, carry):
+        gather(slot, slot).wait_send()
+        returned(slot, slot).wait()
         return carry
 
-    lax.fori_loop(1, 32, return_wait, 0)
+    lax.fori_loop(1, 32, finish, 0)
     gi_ref[...] = (gpart[0] + jnp.sum(grecv[1:].astype(F32), axis=0)).astype(BF16)
 
 
@@ -290,8 +310,8 @@
 
 def per_device(activations, out_grad, w_gate, w_up, w_down):
     depth, width = w_gate.shape
-    cut = (width // 128 + 1) // 2 * 128
-    bounds = ((0, cut), (cut, width))
+    cuts = (0, 384, 640, width)
+    bounds = tuple(zip(cuts, cuts[1:]))
     dma = pltpu.SemaphoreType.DMA
     vmem = pl.BlockSpec(memory_space=pltpu.VMEM)
     hbm = pl.BlockSpec(memory_space=pltpu.MemorySpace.HBM)

time: 92.6 us -> 98.4 us (1.063)
  Pallas kernels: 91.8 us -> 97.6 us
    pallas_call x1, Pallas kernels: 90.7 us -> 96.5 us  [per_device(): pl.pallas_call(functools.partial(kernel, bounds), out_shape=tuple((pltpu....]
where the time goes in v4:
time: 98.4 us; the launch traced here: 98.2 us
  Pallas kernels  97.6 us (99%)
    pallas_call x1, Pallas kernels, per_device(): pl.pallas_call(functools.partial(kernel, bounds), out_shape=tuple((pltpu....  96.5 us

profile of v4, /device:TPU:1, one launch (start us, length us, event | category | flops | bytes accessed | tf_op | source)
XLA Modules:
  0.0 98.2 jit_solution(8219476067544497322)
XLA Ops:
  0.6 96.5 %ffn_backward.1 = (bf16[8,256]{1,0:T(8,128)(2,1)S(1)}, bf16[256,896]{1,0:T(8,128)(2,1)S(1)}, bf16[256,896]{1,0:T(8,128)(2,1)S(1)}, bf16[896,256]{1,0:T(8,128)(2,1)S(1)}) custom-call(bf16[8,256]{1,0:T(8,128)(2,1)} %act_hbm.1, bf16[8,256]{1,0:T(8,128)(2,1)} %og_hbm.1, bf16[256,896]{1,0:T(8,128)(2,1)} %wg_hbm.1, bf16[256,896]{1,0:T(8,128)(2,1)} %wu_hbm.1, ...), custom_call_target="tpu_custom_call" | custom-call | tf_op jit(solution)/shard_map/ffn_backward/pallas_call | solution.py:338
  97.1 1.1 %deliver.1 = (bf16[8,256]{1,0:T(8,128)(2,1)}, bf16[256,896]{1,0:T(8,128)(2,1)}, bf16[256,896]{1,0:T(8,128)(2,1)}, bf16[896,256]{1,0:T(8,128)(2,1)}) custom-call(bf16[8,256]{1,0:T(8,128)(2,1)S(1)} %get-tuple-element.8.refs_0_, bf16[256,896]{1,0:T(8,128)(2,1)S(1)} %get-tuple-element.9.refs_1_, bf16[256,896]{1,0:T(8,128)(2,1)S(1)} %get-tuple-element.10.refs_2_, ...), custom_call_target="tpu_custom_call" | custom-call | tf_op jit(solution)/shard_map/deliver/pallas_call | solution.py:364

commit v5 on v3

--- a/solution.py
+++ b/solution.py
@@ -14,6 +14,29 @@
 NY, NX, NZ = 8, 4, 8
 LAST_DIMS = (((1,), (1,)), ((), ()))
 FIRST_DIMS = (((0,), (0,)), ((), ()))
+
+
+ORDER = (
+    (0, 0, 4, 0, 1), (0, 0, 3, 1, 1), (0, 1, 4, 0, 1), (0, 0, 3, 0, 3), (0, 0, 4, 1, 2), (0, 0, 4, 0, 0),
+    (0, 1, 3, 1, 1), (0, 0, 3, 1, 0), (0, 0, 3, 0, 2), (0, 1, 4, 1, 2), (0, 0, 3, 0, 1), (0, 0, 4, 1, 3),
+    (0, 1, 3, 0, 1), (0, 1, 3, 0, 2), (0, 0, 3, 1, 2), (0, 0, 2, 0, 3), (0, 0, 2, 1, 1), (0, 0, 3, 0, 0),
+    (0, 1, 3, 1, 0), (0, 0, 2, 0, 2), (0, 1, 3, 1, 2), (0, 0, 2, 1, 0), (0, 0, 2, 0, 1), (0, 1, 4, 1, 3),
+    (0, 1, 2, 1, 1), (0, 1, 4, 0, 0), (0, 0, 2, 1, 2), (0, 1, 2, 0, 1), (0, 0, 1, 1, 1), (0, 0, 2, 0, 0),
+    (0, 1, 2, 1, 0), (0, 0, 3, 1, 3), (0, 0, 1, 0, 1), (0, 1, 3, 1, 3), (0, 1, 1, 1, 1), (0, 1, 3, 0, 0),
+    (0, 0, 1, 1, 2), (0, 1, 2, 1, 2), (0, 0, 1, 0, 2), (0, 1, 1, 0, 1), (0, 1, 2, 0, 2), (1, 0, 1), (0, 0, 1, 1, 0),
+    (0, 1, 2, 0, 0), (0, 0, 1, 0, 0), (0, 0, 2, 1, 3), (0, 1, 3, 0, 3), (0, 1, 1, 1, 0), (1, 1, 1), (0, 1, 1, 1, 2),
+    (0, 1, 1, 0, 2), (1, 0, 2), (0, 1, 1, 0, 0), (0, 1, 2, 1, 3), (1, 0, 0), (0, 1, 2, 0, 3), (0, 0, 1, 1, 3),
+    (0, 0, 1, 0, 3), (1, 1, 0), (1, 1, 2), (0, 1, 1, 0, 3), (0, 1, 1, 1, 3), (1, 0, 3), (2, 0), (1, 1, 3), (2, 1),
+    (3, 0, 2, 1, 0), (3, 0, 2, 0, 0), (3, 0, 1, 1, 3), (3, 0, 1, 0, 1), (3, 0, 1, 1, 1), (3, 0, 1, 0, 3),
+    (3, 1, 2, 1, 0), (3, 0, 1, 0, 2), (3, 0, 1, 1, 2), (3, 1, 1, 0, 3), (3, 1, 1, 0, 1), (3, 1, 1, 1, 1),
+    (3, 1, 1, 1, 3), (3, 0, 2, 1, 3), (3, 0, 2, 0, 1), (3, 1, 1, 1, 2), (3, 1, 1, 0, 2), (3, 0, 2, 0, 3),
+    (3, 1, 2, 0, 0), (3, 0, 2, 1, 1), (3, 0, 3, 0, 0), (3, 0, 2, 1, 2), (3, 1, 2, 0, 3), (3, 1, 2, 0, 1),
+    (3, 1, 2, 1, 3), (3, 1, 2, 1, 1), (3, 0, 3, 1, 3), (3, 0, 2, 0, 2), (3, 0, 3, 0, 1), (3, 1, 2, 1, 2),
+    (3, 1, 3, 0, 0), (3, 0, 3, 1, 1), (3, 1, 2, 0, 2), (3, 1, 3, 1, 3), (3, 1, 3, 0, 3), (3, 0, 3, 1, 2),
+    (3, 1, 3, 1, 0), (3, 1, 3, 0, 1), (3, 0, 4, 0, 0), (3, 1, 3, 1, 1), (3, 1, 3, 1, 2), (3, 0, 4, 0, 1),
+    (3, 0, 4, 1, 3), (3, 0, 3, 0, 2), (3, 1, 4, 0, 0), (3, 0, 3, 1, 0), (3, 1, 4, 1, 3), (3, 0, 3, 0, 3),
+    (3, 0, 4, 1, 2), (3, 1, 4, 0, 1), (3, 1, 3, 0, 2), (3, 1, 4, 1, 2),
+)
 
 
 def flat(value):
@@ -38,22 +61,24 @@
     *parts,
 ):
     row, col = lax.axis_index("row"), lax.axis_index("col")
-    y, xh = row // NX, row % NX
-    xl, z, core = col // (2 * NZ), (col // 2) % NZ, col % 2
-    mine = y * NX + xh
+    y, xh = row >> 2, row & 3
+    xl, z, core = col >> 4, (col >> 1) & 7, col & 1
+    mine = row
+    ys, xs = [((y + dy) & 7) << 2 for dy in range(NY)], [(xh + dx) & 3 for dx in range(NX)]
+    blocks_at = [[yy + xx for xx in xs] for yy in ys]
     halves = [parts[7 * h : 7 * h + 7] for h in range(len(bounds))]
 
     def col_id(dx, dz, dc):
-        return (row, ((xl + dx) % 2) * (2 * NZ) + ((z + dz) % NZ) * 2 + (core + dc) % 2)
+        return (row, (((xl + dx) & 1) << 4) + (((z + dz) & 7) << 1) + ((core + dc) & 1))
 
     def slot_id(slot):
-        return col_id(slot // (2 * NZ), (slot // 2) % NZ, slot % 2)
+        return col_id(slot >> 4, (slot >> 1) & 7, slot & 1)
 
     def slot_there(slot):
-        return slot // (2 * NZ) * (2 * NZ) + (NZ - (slot // 2) % NZ) % NZ * 2 + slot % 2
+        return (slot & 17) + (((NZ - ((slot >> 1) & 7)) & 7) << 1)
 
     def row_id(dy, dx):
-        return (((y + dy) % NY) * NX + (xh + dx) % NX, col)
+        return (blocks_at[dy % NY][dx % NX], col)
 
     sent = []
 
@@ -129,24 +154,17 @@
             row_id(1 if side == 0 else NY - 1, 0), start,
         )
 
-    def hop(h, k, near=True, distant=True):
+    def hop(h, k, side, t):
         part, out16, _, out32, _, _, _ = halves[h]
-        order = [(side, t) for t in range(NX) for side in (0, 1)]
-        if k > 1:
-            order = [p for p in order if not far(*p)] + [p for p in order if far(*p)]
-        for side, t in order:
-            if (k == 4 and not far(side, t)) or not (distant if far(side, t) else near):
-                continue
-            block = ((y + (k if side == 0 else NY - k)) % NY) * NX + (xh + 1 + t) % NX
-            value = part[block]
-            if k <= 2 or (k == 3 and far(side, t)):
-                chain(h, side, k + 1, t, start=False).wait_recv()
-                value += chain_in(h, side, k + 1, t)[...].astype(F32)
-            if narrow(side, k, t):
-                out16[side, k - 2, t] = value.astype(BF16)
-            else:
-                out32[side, k - 1, t] = value
-            chain(h, side, k, t)
+        value = part[blocks_at[(k if side == 0 else NY - k) % NY][(1 + t) % NX]]
+        if k <= 2 or (k == 3 and far(side, t)):
+            chain(h, side, k + 1, t, start=False).wait_recv()
+            value += chain_in(h, side, k + 1, t)[...].astype(F32)
+        if narrow(side, k, t):
+            out16[side, k - 2, t] = value.astype(BF16)
+        else:
+            out32[side, k - 1, t] = value
+        chain(h, side, k, t)
 
     def cross(h, t, there, start=True):
         _, _, _, out32, _, xin, _ = halves[h]
@@ -154,14 +172,13 @@
             xin.at[0, t], xin.at[1, t], x_send.at[h, t], x_recv.at[h, t], row_id(0, there), start
         )
 
-    def turn(h):
+    def turn(h, t):
         part, _, _, _, in32, xin, _ = halves[h]
-        for t in range(NX):
-            for side in (0, 1):
-                chain(h, side, 1, t, start=False).wait_recv()
-            xin[0, t] = in32[0, 0, t] + in32[1, 0, t] + part[y * NX + (xh + 1 + t) % NX]
-            if t < NX - 1:
-                cross(h, t, 1 + t)
+        for side in (0, 1):
+            chain(h, side, 1, t, start=False).wait_recv()
+        xin[0, t] = in32[0, 0, t] + in32[1, 0, t] + part[blocks_at[0][(1 + t) % NX]]
+        if t < NX - 1:
+            cross(h, t, 1 + t)
 
     def share(h, t, block, start=True):
         hbuf = halves[h][6]
@@ -177,7 +194,7 @@
         )
 
     def source(side, k, u):
-        return ((y + (NY - k if side == 0 else k)) % NY) * NX + (xh + NX - u) % NX
+        return blocks_at[(NY - k if side == 0 else k) % NY][(NX - u) % NX]
 
     def activate(h):
         _, _, _, _, _, xin, hbuf = halves[h]
@@ -194,19 +211,16 @@
         for t in (0, 2, 1):
             share(h, t, mine)
 
-    def spread(h, k):
-        for u in (0, 1, 3, 2):
-            if k == 1 and u == 0:
-                continue
-            if k == 1:
-                share(h, u - 1, source(0, 0, u), start=False).wait_recv()
-            for side in (0, 1):
-                if k == 4 and not far(side, u):
-                    continue
-                block = source(side, k - 1, u)
-                if k > 1:
-                    forward(h, side, k - 1, u, block, start=False).wait_recv()
-                forward(h, side, k, u, block)
+    shared = set()
+
+    def spread(h, k, side, u):
+        block = source(side, k - 1, u)
+        if k > 1:
+            forward(h, side, k - 1, u, block, start=False).wait_recv()
+        elif (h, u) not in shared:
+            shared.add((h, u))
+            share(h, u - 1, block, start=False).wait_recv()
+        forward(h, side, k, u, block)
 
     def landed(h):
         for u in (0, 1, 3, 2):
@@ -214,29 +228,13 @@
                 last = 4 if far(side, u) else 3
                 forward(h, side, last, u, source(side, last, u), start=False).wait_recv()
 
-    products(0)
-    hop(0, 4)
-    hop(0, 3, distant=False)
-    products(1)
-    hop(0, 3, near=False)
-    hop(1, 4)
-    hop(0, 2)
-    hop(1, 3)
-    hop(0, 1)
-    hop(1, 2)
-    turn(0)
-    hop(1, 1)
-    activate(0)
-    turn(1)
-    spread(0, 1)
-    spread(0, 2)
-    activate(1)
-    spread(0, 3)
-    spread(1, 1)
-    spread(0, 4)
-    spread(1, 2)
-    spread(1, 3)
-    spread(1, 4)
+    steps = (hop, turn, activate, spread)
+    ready = set()
+    for kind, h, *where in ORDER:
+        if h not in ready:
+            ready.add(h)
+            products(h)
+        steps[kind](h, *where)
     landed(0)
     landed(1)
 

time: 92.6 us -> 86 us (0.929)
  Pallas kernels: 91.8 us -> 85.2 us
    pallas_call x1, Pallas kernels: 90.7 us -> 84.1 us  [per_device(): pl.pallas_call(functools.partial(kernel, bounds), out_shape=tuple((pltpu....]
where the time goes in v5:
time: 86 us; the launch traced here: 85.9 us
  Pallas kernels  85.2 us (99%)
    pallas_call x1, Pallas kernels, per_device(): pl.pallas_call(functools.partial(kernel, bounds), out_shape=tuple((pltpu....  84.1 us

profile of v5, /device:TPU:1, one launch (start us, length us, event | category | flops | bytes accessed | tf_op | source)
XLA Modules:
  0.0 85.9 jit_solution(16445725069518620307)
XLA Ops:
  0.6 84.1 %ffn_backward.1 = (bf16[8,256]{1,0:T(8,128)(2,1)S(1)}, bf16[256,896]{1,0:T(8,128)(2,1)S(1)}, bf16[256,896]{1,0:T(8,128)(2,1)S(1)}, bf16[896,256]{1,0:T(8,128)(2,1)S(1)}) custom-call(bf16[8,256]{1,0:T(8,128)(2,1)} %act_hbm.1, bf16[8,256]{1,0:T(8,128)(2,1)} %og_hbm.1, bf16[256,896]{1,0:T(8,128)(2,1)} %wg_hbm.1, bf16[256,896]{1,0:T(8,128)(2,1)} %wu_hbm.1, ...), custom_call_target="tpu_custom_call" | custom-call | tf_op jit(solution)/shard_map/ffn_backward/pallas_call | solution.py:316
  84.8 1.1 %deliver.1 = (bf16[8,256]{1,0:T(8,128)(2,1)}, bf16[256,896]{1,0:T(8,128)(2,1)}, bf16[256,896]{1,0:T(8,128)(2,1)}, bf16[896,256]{1,0:T(8,128)(2,1)}) custom-call(bf16[8,256]{1,0:T(8,128)(2,1)S(1)} %get-tuple-element.8.refs_0_, bf16[256,896]{1,0:T(8,128)(2,1)S(1)} %get-tuple-element.9.refs_1_, bf16[256,896]{1,0:T(8,128)(2,1)S(1)} %get-tuple-element.10.refs_2_, ...), custom_call_target="tpu_custom_call" | custom-call | tf_op jit(solution)/shard_map/deliver/pallas_call | solution.py:342
